TPU v7x, 32 devices: a whole 2x2x4 slice. The times are simulated.
32 devices in a mesh: dp: 8 (over z, y), tensor: 4 (over x, core).
Axes of the slice: x: 2, y: 2, z: 4, core: 2. Of those that a mesh axis runs over, the one named last changes fastest.
Arguments:
- tokens: bfloat16 [16384, 512], P(('dp', 'tensor')), may hold values from -6 to 6
- encoder_states: bfloat16 [16384, 512], P(('dp', 'tensor')), may hold values from -6 to 6
- output_grad: bfloat16 [16384, 512], P(('dp', 'tensor')), may hold values from -6 to 6
- valid_mask: int32 [16384], P(('dp', 'tensor')), may hold values 0 or 1
- segment_ids: int32 [16, 1024], P('dp'), may hold values from 0 to 15, never falling along the last dimension, each value on 1 to 512 neighbouring positions
- context_ranks: int32 [16, 8], P('dp'), may hold values from 0 to 7, each once within a row
- self_query: bfloat16 [512, 512], P('dp', 'tensor'), may hold values from -0.25 to 0.25
- self_key: bfloat16 [512, 512], P('dp', 'tensor'), may hold values from -0.25 to 0.25
- self_value: bfloat16 [512, 512], P('dp', 'tensor'), may hold values from -0.25 to 0.25
- self_output: bfloat16 [512, 512], P('tensor', 'dp'), may hold values from -1.5 to 1.5
- cross_query: bfloat16 [512, 512], P('dp', 'tensor'), may hold values from -0.25 to 0.25
- cross_key: bfloat16 [512, 512], P('dp', 'tensor'), may hold values from -0.25 to 0.25
- cross_value: bfloat16 [512, 512], P('dp', 'tensor'), may hold values from -0.25 to 0.25
- cross_output: bfloat16 [512, 512], P('tensor', 'dp'), may hold values from -4 to 4
- hidden_up: bfloat16 [512, 2048], P('dp', 'tensor'), may hold values from -0.25 to 0.25
- hidden_down: bfloat16 [2048, 512], P('tensor', 'dp'), may hold values from -0.1875 to 0.1875
- norm1_gain: float32 [512], replicated, may hold values from 0.5 to 1.5
- norm1_bias: float32 [512], replicated, may hold values from -1.2 to 1.2
- norm2_gain: float32 [512], replicated, may hold values from 0.5 to 1.5
- norm2_bias: float32 [512], replicated, may hold values from -1.2 to 1.2
- norm3_gain: float32 [512], replicated, may hold values from 0.5 to 1.5
- norm3_bias: float32 [512], replicated, may hold values from -1.2 to 1.2
Outputs:
- layer_output: float32 [16384, 512], P(('dp', 'tensor'))
- tokens_grad: float32 [16384, 512], P(('dp', 'tensor'))
- encoder_grad: float32 [16384, 512], P(('dp', 'tensor'))
- grad_self_query: float32 [512, 512], P('dp', 'tensor')
- grad_self_key: float32 [512, 512], P('dp', 'tensor')
- grad_self_value: float32 [512, 512], P('dp', 'tensor')
- grad_self_output: float32 [512, 512], P('tensor', 'dp')
- grad_cross_query: float32 [512, 512], P('dp', 'tensor')
- grad_cross_key: float32 [512, 512], P('dp', 'tensor')
- grad_cross_value: float32 [512, 512], P('dp', 'tensor')
- grad_cross_output: float32 [512, 512], P('tensor', 'dp')
- grad_hidden_up: float32 [512, 2048], P('dp', 'tensor')
- grad_hidden_down: float32 [2048, 512], P('tensor', 'dp')
- norm_grads: float32 [6, 512], replicated
- valid_scales: float32 [2, 512], replicated
Inputs may be any that keep to these rules, and one draw needn't show every extreme that they name: `segment_ids`: within a sequence the ids never fall; each document has 1 to 512 tokens and one has exactly 512. `context_ranks`: each sequence's row holds every block rank once.
All inputs are finite; a program needn't handle non-finite values. No bound on the sum of `valid_mask` on one device may be relied on, other than what follows from the above.
Results may differ from a plain program's by a relative error of at most 0.024.
The roundings to bfloat16 on the way count: a program that leaves them out, or rounds other values in their place, can miss the bound.
Values may be sent and summed in bfloat16 or wider, within the bound.
A program may use at most 128 MiB of HBM per device.

v0:
```python
import jax
import jax.numpy as jnp
from jax import lax
from jax.sharding import PartitionSpec as P

HEAD = 64
LEN = 1024
BLK = 128
norm_eps = 1e-05
mask_fill = -1000000000.0


def gelu_exact(value):
    return jax.nn.gelu(value, approximate=False)


def gelu_back(preact, upstream):
    return jax.vjp(gelu_exact, preact)[1](upstream)[0]


def layer_norm(value, gain, bias):
    mean = jnp.mean(value, axis=-1, keepdims=True)
    centred = value - mean
    scale = lax.rsqrt(jnp.mean(centred * centred, axis=-1, keepdims=True) + norm_eps)
    normal = centred * scale
    return (normal * gain + bias, normal, scale)


def norm_back(upstream, normal, scale, gain):
    scaled = upstream * gain
    mean_grad = jnp.mean(scaled, axis=-1, keepdims=True)
    mean_cross = jnp.mean(scaled * normal, axis=-1, keepdims=True)
    inward = scale * (scaled - mean_grad - normal * mean_cross)
    return (inward, jnp.sum(upstream * normal, axis=0), jnp.sum(upstream, axis=0))


def context_allowed(segments, ranks, first, count):
    length = segments.shape[0]
    key_block = jnp.arange(length, dtype=jnp.int32) // BLK
    key_rank = jnp.broadcast_to(ranks[:, None], (ranks.shape[0], BLK)).reshape(length)
    query_segment = lax.dynamic_slice_in_dim(segments, first, count)
    query_rank = lax.dynamic_slice_in_dim(key_rank, first, count)
    query_block = (first + jnp.arange(count, dtype=jnp.int32)) // BLK
    same_doc = query_segment[:, None] == segments[None, :]
    earlier = key_rank[None, :] < query_rank[:, None]
    same_block = query_block[:, None] == key_block[None, :]
    return same_doc & (earlier | same_block)


def full_rows(value):
    return lax.all_gather(value, "tensor", axis=0, tiled=True)


def grad_rows(value):
    return lax.all_gather(value, "tensor", axis=0, tiled=True)


def branch_sum(mixed, weight):
    return lax.psum_scatter(
        jnp.dot(mixed, weight, preferred_element_type=jnp.float32),
        "tensor",
        scatter_dimension=0,
        tiled=True,
    )


def back_product(left, weight):
    return lax.dot_general(
        left, weight, (((1,), (1,)), ((), ())), preferred_element_type=jnp.float32
    )


def row_product(left, right):
    return lax.dot_general(
        left, right, (((0,), (0,)), ((), ())), preferred_element_type=jnp.float32
    )


def input_sum(pairs):
    total = None
    for left, weight in pairs:
        portion = back_product(left, weight)
        total = portion if total is None else total + portion
    return lax.psum_scatter(total, "tensor", scatter_dimension=0, tiled=True)


def split_heads(value, count):
    return value.reshape(count, LEN, value.shape[1] // HEAD, HEAD)


def attend_sequence(query, keys, values, segments, ranks, masked):
    length = query.shape[0]
    width = min(length, 512)

    def one_block(index):
        first = index * width
        piece = lax.dynamic_slice_in_dim(query, first, width, 0)
        scores = jnp.einsum("qhd,khd->hqk", piece, keys, preferred_element_type=jnp.float32) * 0.125
        if masked:
            scores = jnp.where(
                context_allowed(segments, ranks, first, width)[None], scores, mask_fill
            )
        top = jnp.max(scores, axis=-1, keepdims=True)
        raised = jnp.exp(scores - top)
        total = jnp.sum(raised, axis=-1, keepdims=True)
        shares = (raised / total).astype(jnp.bfloat16)
        mixed = jnp.einsum("hqk,khd->qhd", shares, values, preferred_element_type=jnp.float32)
        return (mixed.astype(jnp.bfloat16), (top + jnp.log(total))[..., 0])

    mixed, log_total = lax.map(one_block, jnp.arange(length // width, dtype=jnp.int32))
    return (mixed.reshape(query.shape), log_total)


def attend_sequence_back(query, keys, values, segments, ranks, masked, log_total, grad_mixed):
    length = query.shape[0]
    width = min(length, 512)

    def one_block(carry, index):
        key_sum, value_sum = carry
        first = index * width
        piece = lax.dynamic_slice_in_dim(query, first, width, 0)
        grad_piece = lax.dynamic_slice_in_dim(grad_mixed, first, width, 0)
        scores = jnp.einsum("qhd,khd->hqk", piece, keys, preferred_element_type=jnp.float32) * 0.125
        if masked:
            scores = jnp.where(
                context_allowed(segments, ranks, first, width)[None], scores, mask_fill
            )
        shares = jnp.exp(scores - log_total[index][..., None])
        grad_shares = jnp.einsum(
            "qhd,khd->hqk", grad_piece, values, preferred_element_type=jnp.float32
        )
        inner = jnp.sum(shares * grad_shares, axis=-1, keepdims=True)
        grad_scores = (shares * (grad_shares - inner)).astype(jnp.bfloat16)
        grad_query = (
            jnp.einsum("hqk,khd->qhd", grad_scores, keys, preferred_element_type=jnp.float32)
            * 0.125
        )
        key_sum = (
            key_sum
            + jnp.einsum("hqk,qhd->khd", grad_scores, piece, preferred_element_type=jnp.float32)
            * 0.125
        )
        value_sum = value_sum + jnp.einsum(
            "hqk,qhd->khd",
            shares.astype(jnp.bfloat16),
            grad_piece,
            preferred_element_type=jnp.float32,
        )
        return ((key_sum, value_sum), grad_query.astype(jnp.bfloat16))

    zeros = jnp.zeros(keys.shape, jnp.float32)
    (key_sum, value_sum), grad_query = lax.scan(
        one_block, (zeros, zeros), jnp.arange(length // width, dtype=jnp.int32)
    )
    return (
        grad_query.reshape(query.shape),
        key_sum.astype(jnp.bfloat16),
        value_sum.astype(jnp.bfloat16),
    )


def attend_all(query, keys, values, segments, ranks, masked):
    count = query.shape[0] // LEN

    def one_sequence(items):
        return attend_sequence(items[0], items[1], items[2], items[3], items[4], masked)

    mixed, log_total = lax.map(
        one_sequence,
        (
            split_heads(query, count),
            split_heads(keys, count),
            split_heads(values, count),
            segments,
            ranks,
        ),
    )
    return (mixed.reshape(query.shape), log_total)


def attend_back_all(query, keys, values, segments, ranks, masked, log_total, grad_mixed):
    count = query.shape[0] // LEN

    def one_sequence(items):
        return attend_sequence_back(
            items[0], items[1], items[2], items[3], items[4], masked, items[5], items[6]
        )

    grad_query, grad_keys, grad_values = lax.map(
        one_sequence,
        (
            split_heads(query, count),
            split_heads(keys, count),
            split_heads(values, count),
            segments,
            ranks,
            log_total,
            split_heads(grad_mixed, count),
        ),
    )
    return (
        grad_query.reshape(query.shape),
        grad_keys.reshape(keys.shape),
        grad_values.reshape(values.shape),
    )


def shards(
    tokens,
    encoder_states,
    output_grad,
    valid_mask,
    segment_ids,
    context_ranks,
    self_query,
    self_key,
    self_value,
    self_output,
    cross_query,
    cross_key,
    cross_value,
    cross_output,
    hidden_up,
    hidden_down,
    norm1_gain,
    norm1_bias,
    norm2_gain,
    norm2_bias,
    norm3_gain,
    norm3_bias,
):
    (
        self_query,
        self_key,
        self_value,
        self_output,
        cross_query,
        cross_key,
        cross_value,
        cross_output,
        hidden_up,
        hidden_down,
    ) = (
        lax.all_gather(self_query, "dp", axis=0, tiled=True),
        lax.all_gather(self_key, "dp", axis=0, tiled=True),
        lax.all_gather(self_value, "dp", axis=0, tiled=True),
        lax.all_gather(self_output, "dp", axis=1, tiled=True),
        lax.all_gather(cross_query, "dp", axis=0, tiled=True),
        lax.all_gather(cross_key, "dp", axis=0, tiled=True),
        lax.all_gather(cross_value, "dp", axis=0, tiled=True),
        lax.all_gather(cross_output, "dp", axis=1, tiled=True),
        lax.all_gather(hidden_up, "dp", axis=0, tiled=True),
        lax.all_gather(hidden_down, "dp", axis=1, tiled=True),
    )
    tokens_full = full_rows(tokens)
    query = jnp.dot(tokens_full, self_query, preferred_element_type=jnp.float32).astype(
        jnp.bfloat16
    )
    keys = jnp.dot(tokens_full, self_key, preferred_element_type=jnp.float32).astype(jnp.bfloat16)
    values = jnp.dot(tokens_full, self_value, preferred_element_type=jnp.float32).astype(
        jnp.bfloat16
    )
    self_mixed, self_log = attend_all(query, keys, values, segment_ids, context_ranks, True)
    attended = branch_sum(self_mixed, self_output)
    first_out, first_normal, first_scale = layer_norm(
        tokens.astype(jnp.float32) + attended, norm1_gain, norm1_bias
    )
    first_full = full_rows(first_out.astype(jnp.bfloat16))
    encoder_full = full_rows(encoder_states)
    second_query = jnp.dot(first_full, cross_query, preferred_element_type=jnp.float32).astype(
        jnp.bfloat16
    )
    encoder_keys = jnp.dot(encoder_full, cross_key, preferred_element_type=jnp.float32).astype(
        jnp.bfloat16
    )
    encoder_values = jnp.dot(encoder_full, cross_value, preferred_element_type=jnp.float32).astype(
        jnp.bfloat16
    )
    cross_mixed, cross_log = attend_all(
        second_query, encoder_keys, encoder_values, segment_ids, context_ranks, False
    )
    crossed = branch_sum(cross_mixed, cross_output)
    second_out, second_normal, second_scale = layer_norm(
        first_out + crossed, norm2_gain, norm2_bias
    )
    second_low = second_out.astype(jnp.bfloat16)
    feed_input = full_rows(second_low)
    preact = jnp.dot(feed_input, hidden_up, preferred_element_type=jnp.float32)
    activated = gelu_exact(preact).astype(jnp.bfloat16)
    feed_out = branch_sum(activated, hidden_down)
    third_out, third_normal, third_scale = layer_norm(second_out + feed_out, norm3_gain, norm3_bias)
    valid_rows = valid_mask.astype(jnp.float32)[:, None]
    grad_layer = output_grad.astype(jnp.float32) * valid_rows
    grad_third, gain3_grad, bias3_grad = norm_back(
        grad_layer, third_normal, third_scale, norm3_gain
    )
    grad_third_low = grad_third.astype(jnp.bfloat16)
    grad_feed = grad_rows(grad_third_low)
    grad_active = back_product(grad_feed, hidden_down)
    grad_preact = gelu_back(preact, grad_active).astype(jnp.bfloat16)
    up_grad = row_product(feed_input, grad_preact)
    down_grad = row_product(activated, grad_feed)
    grad_second = grad_third + input_sum([(grad_preact, hidden_up)])
    grad_second_in, gain2_grad, bias2_grad = norm_back(
        grad_second, second_normal, second_scale, norm2_gain
    )
    grad_crossed = grad_rows(grad_second_in.astype(jnp.bfloat16))
    cross_output_grad = row_product(cross_mixed, grad_crossed)
    grad_cross_mixed = back_product(grad_crossed, cross_output).astype(jnp.bfloat16)
    grad_second_query, grad_encoder_keys, grad_encoder_values = attend_back_all(
        second_query,
        encoder_keys,
        encoder_values,
        segment_ids,
        context_ranks,
        False,
        cross_log,
        grad_cross_mixed,
    )
    cross_query_grad = row_product(first_full, grad_second_query)
    cross_key_grad = row_product(encoder_full, grad_encoder_keys)
    cross_value_grad = row_product(encoder_full, grad_encoder_values)
    grad_first = grad_second_in + input_sum([(grad_second_query, cross_query)])
    encoder_grad = input_sum([(grad_encoder_keys, cross_key), (grad_encoder_values, cross_value)])
    grad_first_in, gain1_grad, bias1_grad = norm_back(
        grad_first, first_normal, first_scale, norm1_gain
    )
    grad_attended = grad_rows(grad_first_in.astype(jnp.bfloat16))
    self_output_grad = row_product(self_mixed, grad_attended)
    grad_self_mixed = back_product(grad_attended, self_output).astype(jnp.bfloat16)
    grad_query, grad_keys, grad_values = attend_back_all(
        query, keys, values, segment_ids, context_ranks, True, self_log, grad_self_mixed
    )
    self_query_grad = row_product(tokens_full, grad_query)
    self_key_grad = row_product(tokens_full, grad_keys)
    self_value_grad = row_product(tokens_full, grad_values)
    tokens_grad = grad_first_in + input_sum(
        [(grad_query, self_query), (grad_keys, self_key), (grad_values, self_value)]
    )
    (
        self_query_grad,
        self_key_grad,
        self_value_grad,
        self_output_grad,
        cross_query_grad,
        cross_key_grad,
        cross_value_grad,
        cross_output_grad,
        up_grad,
        down_grad,
    ) = (
        lax.psum_scatter(self_query_grad, "dp", scatter_dimension=0, tiled=True),
        lax.psum_scatter(self_key_grad, "dp", scatter_dimension=0, tiled=True),
        lax.psum_scatter(self_value_grad, "dp", scatter_dimension=0, tiled=True),
        lax.psum_scatter(self_output_grad, "dp", scatter_dimension=1, tiled=True),
        lax.psum_scatter(cross_query_grad, "dp", scatter_dimension=0, tiled=True),
        lax.psum_scatter(cross_key_grad, "dp", scatter_dimension=0, tiled=True),
        lax.psum_scatter(cross_value_grad, "dp", scatter_dimension=0, tiled=True),
        lax.psum_scatter(cross_output_grad, "dp", scatter_dimension=1, tiled=True),
        lax.psum_scatter(up_grad, "dp", scatter_dimension=0, tiled=True),
        lax.psum_scatter(down_grad, "dp", scatter_dimension=1, tiled=True),
    )
    norm_sums, square_sums = lax.psum(
        (
            jnp.stack([gain1_grad, bias1_grad, gain2_grad, bias2_grad, gain3_grad, bias3_grad]),
            jnp.stack(
                [
                    jnp.sum(valid_rows * third_out * third_out, axis=0),
                    jnp.sum(valid_rows * tokens_grad * tokens_grad, axis=0),
                ]
            ),
        ),
        ("dp", "tensor"),
    )
    total_tokens = tokens.shape[0] * lax.axis_size("dp") * lax.axis_size("tensor")
    valid_scales = jnp.sqrt(square_sums / total_tokens)
    return (
        third_out,
        tokens_grad,
        encoder_grad,
        self_query_grad,
        self_key_grad,
        self_value_grad,
        self_output_grad,
        cross_query_grad,
        cross_key_grad,
        cross_value_grad,
        cross_output_grad,
        up_grad,
        down_grad,
        norm_sums,
        valid_scales,
    )


def solution(mesh):
    in_specs = (
        P(("dp", "tensor"), None),
        P(("dp", "tensor"), None),
        P(("dp", "tensor"), None),
        P(("dp", "tensor")),
        P("dp", None),
        P("dp", None),
        P("dp", "tensor"),
        P("dp", "tensor"),
        P("dp", "tensor"),
        P("tensor", "dp"),
        P("dp", "tensor"),
        P("dp", "tensor"),
        P("dp", "tensor"),
        P("tensor", "dp"),
        P("dp", "tensor"),
        P("tensor", "dp"),
        P(),
        P(),
        P(),
        P(),
        P(),
        P(),
    )
    out_specs = (
        P(("dp", "tensor"), None),
        P(("dp", "tensor"), None),
        P(("dp", "tensor"), None),
        P("dp", "tensor"),
        P("dp", "tensor"),
        P("dp", "tensor"),
        P("tensor", "dp"),
        P("dp", "tensor"),
        P("dp", "tensor"),
        P("dp", "tensor"),
        P("tensor", "dp"),
        P("dp", "tensor"),
        P("tensor", "dp"),
        P(),
        P(),
    )
    return jax.shard_map(shards, mesh=mesh, in_specs=in_specs, out_specs=out_specs, check_vma=False)
```

profile of v0, /device:TPU:0, one launch (start us, length us, event | category | flops | bytes accessed | tf_op | source)
XLA Modules:
  0.0 1633.0 jit_solution(10567116157558251906)
XLA Ops:
  8.0 32.6 %all_gather.52 = bf16[512,128]{1,0:T(8,128)(2,1)S(1)} all-gather(bf16[64,128]{1,0:T(8,128)(2,1)} %param.44), channel_id=1, replica_groups=mesh['dp'=8,'tensor'=4] {'dp'}, dimensions={0}, use_global_device_ids=true | all-gather | bytes 147456 | tf_op jit(solution)/shard_map/all_gather | solution.py:244
  40.6 30.8 %all_gather.53 = bf16[512,128]{1,0:T(8,128)(2,1)S(1)} all-gather(bf16[64,128]{1,0:T(8,128)(2,1)} %param.45), channel_id=1, replica_groups=mesh['dp'=8,'tensor'=4] {'dp'}, dimensions={0}, use_global_device_ids=true | all-gather | bytes 147456 | tf_op jit(solution)/shard_map/all_gather | solution.py:245
  102.1 32.7 %all_gather.55 = bf16[128,512]{0,1:T(8,128)(2,1)} all-gather(bf16[128,64]{0,1:T(8,128)(2,1)} %param.47), channel_id=1, replica_groups=mesh['dp'=8,'tensor'=4] {'dp'}, dimensions={1}, use_global_device_ids=true | all-gather | bytes 147456 | tf_op jit(solution)/shard_map/all_gather | solution.py:247
  186.1 44.5 %reduce-scatter.28.cloned.1.call-done = f32[512,512]{1,0:T(8,128)} async-done(((f32[2048,512]{1,0:T(8,128)}), f32[512,512]{1,0:T(8,128)}) %reduce-scatter.28.cloned.1.call-update) | async-done | bytes 1048592 | tf_op jit(solution)/shard_map/reduce_scatter | solution.py:59
  326.3 32.5 %all_gather.61 = bf16[128,512]{0,1:T(8,128)(2,1)} all-gather(bf16[128,64]{0,1:T(8,128)(2,1)S(1)} %copy-done.77), channel_id=1, replica_groups=mesh['dp'=8,'tensor'=4] {'dp'}, dimensions={1}, use_global_device_ids=true | all-gather | bytes 147456 | tf_op jit(solution)/shard_map/all_gather | solution.py:251
  397.9 44.6 %reduce-scatter.30.cloned.1.call-done = f32[512,512]{1,0:T(8,128)} async-done(((f32[2048,512]{1,0:T(8,128)}), f32[512,512]{1,0:T(8,128)}) %reduce-scatter.30.cloned.1.call-update) | async-done | bytes 1048592 | tf_op jit(solution)/shard_map/reduce_scatter | solution.py:59
  445.6 31.4 %all_gather.63 = bf16[512,512]{1,0:T(8,128)(2,1)S(1)} all-gather(bf16[64,512]{1,0:T(8,128)(2,1)S(1)} %copy-done.59), channel_id=1, replica_groups=mesh['dp'=8,'tensor'=4] {'dp'}, dimensions={0}, use_global_device_ids=true | all-gather | bytes 589824 | tf_op jit(solution)/shard_map/all_gather | solution.py:252
  477.0 31.7 %all_gather.64 = bf16[512,512]{0,1:T(8,128)(2,1)S(1)} all-gather(bf16[512,64]{0,1:T(8,128)(2,1)S(1)} %copy-done.60), channel_id=1, replica_groups=mesh['dp'=8,'tensor'=4] {'dp'}, dimensions={1}, use_global_device_ids=true | all-gather | bytes 589824 | tf_op jit(solution)/shard_map/all_gather | solution.py:253
  527.0 44.2 %reduce-scatter.32.cloned.1.call-done = f32[512,512]{1,0:T(8,128)} async-done(((f32[2048,512]{1,0:T(8,128)}), f32[512,512]{1,0:T(8,128)}) %reduce-scatter.32.cloned.1.call-update) | async-done | bytes 1048592 | tf_op jit(solution)/shard_map/reduce_scatter | solution.py:59
  611.9 44.6 %reduce-scatter.34.cloned.1.call-done = f32[512,512]{1,0:T(8,128)} async-done(((f32[2048,512]{1,0:T(8,128)}), f32[512,512]{1,0:T(8,128)}) %reduce-scatter.34.cloned.1.call-update) | async-done | bytes 1048592 | tf_op jit(solution)/shard_map/reduce_scatter | solution.py:84
  691.4 45.9 %while.151 = (s32[]{:T(128)}, bf16[2,1024,2,64]{3,2,1,0:T(2,128)(2,1)}, bf16[2,1024,2,64]{1,3,2,0:T(8,128)(2,1)}, bf16[2,1024,2,64]{1,3,2,0:T(8,128)(2,1)}, bf16...) while((s32[]{:T(128)}, ...), condition=%wide.region_30.31_spmd, body=%wide.region_26.30_spmd.sunk | while | flops 684719104 | bytes 40022608 | solution.py:189
  742.6 44.6 %reduce-scatter.36.cloned.1.call-done = f32[512,512]{1,0:T(8,128)} async-done(((f32[2048,512]{1,0:T(8,128)}), f32[512,512]{1,0:T(8,128)}) %reduce-scatter.36.cloned.1.call-update) | async-done | bytes 1048592 | tf_op jit(solution)/shard_map/reduce_scatter | solution.py:84
  822.1 51.9 %while.153 = (s32[]{:T(128)}, bf16[2,1024,2,64]{3,2,1,0:T(2,128)(2,1)}, bf16[2,1024,2,64]{1,3,2,0:T(8,128)(2,1)}, bf16[2,1024,2,64]{1,3,2,0:T(8,128)(2,1)}, bf16...) while((s32[]{:T(128)}, ...), condition=%wide.region_38.39_spmd, body=%wide.region_34.38_spmd.sunk | while | flops 690502656 | bytes 46359340 | solution.py:189
  932.8 39.9 %all-reduce = (f32[6,512]{1,0:T(8,128)}, f32[2,512]{1,0:T(2,128)S(1)}) all-reduce(f32[6,512]{1,0:T(8,128)S(1)} %stack.36, f32[2,512]{1,0:T(2,128)S(1)} %pad_maximum_fusion), channel_id=1, replica_groups=mesh['dp'=8,'tensor'=4] {'dp','tensor'}, use_global_device_ids=true, to_apply=%region_57.58 | all-reduce | flops 4096 | bytes 32768 | tf_op jit(solution)/shard_map/psum | solution.py:363
  996.8 66.7 %reduce-scatter.50.cloned.1.call-done = f32[512,64]{0,1:T(8,128)} async-done(((f32[512,512]{0,1:T(8,128)}), f32[512,64]{0,1:T(8,128)}) %reduce-scatter.50.cloned.1.call-update) | async-done | bytes 131088 | tf_op jit(solution)/shard_map/reduce_scatter | solution.py:361
  1063.6 64.1 %reduce-scatter.46.cloned.1.call-done = f32[128,64]{0,1:T(8,128)} async-done(((f32[128,512]{0,1:T(8,128)}), f32[128,64]{0,1:T(8,128)}) %reduce-scatter.46.cloned.1.call-update) | async-done | bytes 32784 | tf_op jit(solution)/shard_map/reduce_scatter | solution.py:359
  1127.6 64.1 %reduce-scatter.60.cloned.1.call-done = f32[64,128]{1,0:T(8,128)} async-done(((f32[512,128]{1,0:T(8,128)}), f32[64,128]{1,0:T(8,128)}) %reduce-scatter.60.cloned.1.call-update) | async-done | bytes 32784
  1191.7 64.1 %reduce-scatter.44.cloned.1.call-done = f32[64,128]{1,0:T(8,128)} async-done(((f32[512,128]{1,0:T(8,128)}), f32[64,128]{1,0:T(8,128)}) %reduce-scatter.44.cloned.1.call-update) | async-done | bytes 32784 | tf_op jit(solution)/shard_map/reduce_scatter | solution.py:356
  1255.8 64.2 %reduce-scatter.58.cloned.1.call-done = f32[64,128]{1,0:T(8,128)} async-done(((f32[512,128]{1,0:T(8,128)}), f32[64,128]{1,0:T(8,128)}) %reduce-scatter.58.cloned.1.call-update) | async-done | bytes 32784
  1320.0 46.5 %reduce-scatter.40.cloned.1.call-done = f32[512,512]{1,0:T(8,128)} async-done(((f32[2048,512]{1,0:T(8,128)}), f32[512,512]{1,0:T(8,128)}) %reduce-scatter.40.cloned.1.call-update) | async-done | bytes 1048592 | tf_op jit(solution)/shard_map/reduce_scatter | solution.py:84
  1366.5 65.6 %reduce-scatter.42.cloned.1.call-done = f32[128,64]{0,1:T(8,128)} async-done(((f32[128,512]{0,1:T(8,128)}), f32[128,64]{0,1:T(8,128)}) %reduce-scatter.42.cloned.1.call-update) | async-done | bytes 32784 | tf_op jit(solution)/shard_map/reduce_scatter | solution.py:355
  1432.1 64.6 %reduce-scatter.56.cloned.1.call-done = f32[64,128]{1,0:T(8,128)} async-done(((f32[512,128]{1,0:T(8,128)}), f32[64,128]{1,0:T(8,128)}) %reduce-scatter.56.cloned.1.call-update) | async-done | bytes 32784
  1496.7 64.6 %reduce-scatter.52.cloned.1.call-done = f32[64,128]{1,0:T(8,128)} async-done(((f32[512,128]{1,0:T(8,128)}), f32[64,128]{1,0:T(8,128)}) %reduce-scatter.52.cloned.1.call-update) | async-done | bytes 32784
  1561.3 64.4 %reduce-scatter.54.cloned.1.call-done = f32[64,128]{1,0:T(8,128)} async-done(((f32[512,128]{1,0:T(8,128)}), f32[64,128]{1,0:T(8,128)}) %reduce-scatter.54.cloned.1.call-update) | async-done | bytes 32784
  (608 shorter events, 674.7 us)
Async XLA Ops:
  7.2 127.6 %all-gather.8.cloned.1.call-start = ((), (), s32[]{:S(2)}) async-start(), calls=%async_computation.17 | async-start | bytes 2621440 | tf_op jit(solution)/shard_map/all_gather | solution.py:51
  7.9 222.7 %reduce-scatter.28.cloned.1.call-start = ((), (), s32[]{:S(2)}) async-start(), calls=%async_computation.18 | async-start | bytes 5242880 | tf_op jit(solution)/shard_map/reduce_scatter | solution.py:59
  185.1 173.7 %all-gather.12.cloned.1.call-start = ((), (), s32[]{:S(2)}) async-start(), calls=%async_computation.20 | async-start | bytes 2621440 | tf_op jit(solution)/shard_map/all_gather | solution.py:51
  185.8 182.2 %all-gather.10.cloned.1.call-start = ((), (), s32[]{:S(2)}) async-start(), calls=%async_computation.19 | async-start | bytes 2621440 | tf_op jit(solution)/shard_map/all_gather | solution.py:51
  234.6 208.0 %reduce-scatter.30.cloned.1.call-start = ((), (), s32[]{:S(2)}) async-start(), calls=%async_computation.21 | async-start | bytes 5242880 | tf_op jit(solution)/shard_map/reduce_scatter | solution.py:59
  397.9 110.8 %all-gather.14.cloned.1.call-start = ((), (), s32[]{:S(2)}) async-start(), calls=%async_computation.22 | async-start | bytes 2621440 | tf_op jit(solution)/shard_map/all_gather | solution.py:51
  445.5 125.7 %reduce-scatter.32.cloned.1.call-start = ((), (), s32[]{:S(2)}) async-start(), calls=%async_computation.23 | async-start | bytes 5242880 | tf_op jit(solution)/shard_map/reduce_scatter | solution.py:59
  526.4 74.1 %all-gather.16.cloned.1.call-start = ((), (), s32[]{:S(2)}) async-start(), calls=%async_computation.24 | async-start | bytes 2621440 | tf_op jit(solution)/shard_map/all_gather | solution.py:55
  577.7 78.8 %reduce-scatter.34.cloned.1.call-start = ((), (), s32[]{:S(2)}) async-start(), calls=%async_computation.25 | async-start | bytes 5242880 | tf_op jit(solution)/shard_map/reduce_scatter | solution.py:84
  611.8 71.8 %all-gather.18.cloned.1.call-start = ((), (), s32[]{:S(2)}) async-start(), calls=%async_computation.26 | async-start | bytes 2621440 | tf_op jit(solution)/shard_map/all_gather | solution.py:55
  660.9 126.4 %reduce-scatter.36.cloned.1.call-start = ((), (), s32[]{:S(2)}) async-start(), calls=%async_computation.27 | async-start | bytes 5242880 | tf_op jit(solution)/shard_map/reduce_scatter | solution.py:84
  742.6 71.4 %all-gather.20.cloned.1.call-start = ((), (), s32[]{:S(2)}) async-start(), calls=%async_computation.28 | async-start | bytes 2621440 | tf_op jit(solution)/shard_map/all_gather | solution.py:55
  791.3 138.1 %reduce-scatter.38.cloned.1.call-start = ((), (), s32[]{:S(2)}) async-start(), calls=%async_computation.29 | async-start | bytes 5242880 | tf_op jit(solution)/shard_map/reduce_scatter | solution.py:84
  884.8 112.1 %reduce-scatter.48.cloned.1.call-start = ((), (), s32[]{:S(2)}) async-start(), calls=%async_computation.34 | async-start | bytes 1179648 | tf_op jit(solution)/shard_map/reduce_scatter | solution.py:360
  889.7 173.8 %reduce-scatter.50.cloned.1.call-start = ((), (), s32[]{:S(2)}) async-start(), calls=%async_computation.35 | async-start | bytes 1179648 | tf_op jit(solution)/shard_map/reduce_scatter | solution.py:361
  894.1 233.6 %reduce-scatter.46.cloned.1.call-start = ((), (), s32[]{:S(2)}) async-start(), calls=%async_computation.33 | async-start | bytes 294912 | tf_op jit(solution)/shard_map/reduce_scatter | solution.py:359
  897.6 294.0 %reduce-scatter.60.cloned.1.call-start = ((), (), s32[]{:S(2)}) async-start(), calls=%async_computation.40 | async-start | bytes 294912
  900.7 355.0 %reduce-scatter.44.cloned.1.call-start = ((), (), s32[]{:S(2)}) async-start(), calls=%async_computation.32 | async-start | bytes 294912 | tf_op jit(solution)/shard_map/reduce_scatter | solution.py:356
  903.9 416.1 %reduce-scatter.58.cloned.1.call-start = ((), (), s32[]{:S(2)}) async-start(), calls=%async_computation.39 | async-start | bytes 294912
  908.7 457.8 %reduce-scatter.40.cloned.1.call-start = ((), (), s32[]{:S(2)}) async-start(), calls=%async_computation.30 | async-start | bytes 5242880 | tf_op jit(solution)/shard_map/reduce_scatter | solution.py:84
  912.4 519.7 %reduce-scatter.42.cloned.1.call-start = ((), (), s32[]{:S(2)}) async-start(), calls=%async_computation.31 | async-start | bytes 294912 | tf_op jit(solution)/shard_map/reduce_scatter | solution.py:355
  916.7 580.0 %reduce-scatter.56.cloned.1.call-start = ((), (), s32[]{:S(2)}) async-start(), calls=%async_computation.38 | async-start | bytes 294912
  918.1 643.1 %reduce-scatter.52.cloned.1.call-start = ((), (), s32[]{:S(2)}) async-start(), calls=%async_computation.36 | async-start | bytes 294912
  920.6 705.1 %reduce-scatter.54.cloned.1.call-start = ((), (), s32[]{:S(2)}) async-start(), calls=%async_computation.37 | async-start | bytes 294912
  (97 other events, 2694.9 us)
Sparse Core Ops, SparseCore 0:
  9.6 25.2 all-gather.7
  185.1 45.3 reduce-scatter.27
  232.2 22.5 all-gather.11
  256.9 22.5 all-gather.9
  398.0 44.5 reduce-scatter.29
  445.6 22.5 all-gather.13
  526.5 44.6 reduce-scatter.31
  577.8 22.5 all-gather.15
  611.9 44.5 reduce-scatter.33
  661.0 22.5 all-gather.17
  742.7 44.5 reduce-scatter.35
  791.4 22.5 all-gather.19
  884.9 44.4 reduce-scatter.37
  933.2 63.5 reduce-scatter.47
  1001.0 62.4 reduce-scatter.49
  1067.3 60.2 reduce-scatter.45
  1131.4 60.2 reduce-scatter.59
  1195.4 60.2 reduce-scatter.43
  1259.7 60.2 reduce-scatter.57
  1322.9 43.5 reduce-scatter.39
  1370.8 61.2 reduce-scatter.41
  1436.3 60.2 reduce-scatter.55
  1500.9 60.2 reduce-scatter.51
  1565.4 60.2 reduce-scatter.53
where the time goes:
time: 1640 us; the launch traced here: 1630 us
  waiting for transfers between devices  951 us (58%)
  blocking collectives  354 us (22%)
  matrix products  138 us (8%)
  local copies, waits for them, and re-layouts  91.9 us (6%)
  other arithmetic  53.1 us (3%)
  loops' own time  27.4 us (2%)
    unnamed x29, waiting for transfers between devices  324 us
    reduce_scatter x4, waiting for transfers between devices, input_sum(): return lax.psum_scatter(total, 'tensor', scatter_dimension=0, tiled=True)  142 us
    reduce_scatter x3, waiting for transfers between devices, branch_sum(): lax.psum_scatter(jnp.dot(mixed, weight, preferred_element_type=jnp.float3...  133 us
    all_gather x3, waiting for transfers between devices, grad_rows(): return lax.all_gather(value, 'tensor', axis=0, tiled=True)  67.9 us
    reduce_scatter x1, waiting for transfers between devices, shards(): lax.psum_scatter(down_grad, 'dp', scatter_dimension=1, tiled=True)  66.7 us
    reduce_scatter x1, waiting for transfers between devices, shards(): lax.psum_scatter(self_output_grad, 'dp', scatter_dimension=1, tiled=True)  65.6 us
    reduce_scatter x1, waiting for transfers between devices, shards(): lax.psum_scatter(cross_query_grad, 'dp', scatter_dimension=0, tiled=True)  64.1 us
    reduce_scatter x1, waiting for transfers between devices, shards(): lax.psum_scatter(cross_output_grad, 'dp', scatter_dimension=1, tiled=True)  64.1 us
  transfers between devices with their start and end apart: 24, of which 20 were waited for; matrix products, arithmetic and copies ran while one was open for 3% of the time, Pallas kernels for 0%

commit v1 on v0

--- a/solution.py
+++ b/solution.py
@@ -1,3 +1,4 @@
+import functools
 import jax
 import jax.numpy as jnp
 from jax import lax
@@ -8,6 +9,33 @@
 BLK = 128
 norm_eps = 1e-05
 mask_fill = -1000000000.0
+
+
+def change_trails(raw, chip_axis):
+    g_now = lax.axis_index(chip_axis)
+    block_next = lax.axis_size(chip_axis)
+    side_arr, view_out, right_arr = (block_next, g_now, raw.shape[0])
+    pile = [s * side_arr if u == 0 else s for u, s in enumerate(raw.shape)]
+    fresh = b_now = raw
+    x_next = lax.dynamic_update_slice_in_dim(
+        jnp.zeros(pile, raw.dtype), raw, view_out * right_arr, axis=0
+    )
+    for it in [*range(1, side_arr // 2 + 1)]:
+        fresh = lax.ppermute(fresh, chip_axis, [(u, (u + 1) % side_arr) for u in range(side_arr)])
+        x_next = lax.dynamic_update_slice_in_dim(
+            x_next, fresh, (view_out - it) % side_arr * right_arr, axis=0
+        )
+        if 2 * it < side_arr:
+            b_now = lax.ppermute(
+                b_now, chip_axis, [(u, (u - 1) % side_arr) for u in range(side_arr)]
+            )
+            x_next = lax.dynamic_update_slice_in_dim(
+                x_next, b_now, (view_out + it) % side_arr * right_arr, axis=0
+            )
+    return x_next
+
+
+guide_units = functools.partial(change_trails, chip_axis="tensor")
 
 
 def gelu_exact(value):
@@ -52,7 +80,7 @@
 
 
 def grad_rows(value):
-    return lax.all_gather(value, "tensor", axis=0, tiled=True)
+    return guide_units(value)
 
 
 def branch_sum(mixed, weight):

time: 1640 us -> 1750 us (1.067)
  matrix products: 138 us -> 203 us
  local copies, waits for them, and re-layouts: 91.9 us -> 142 us
    all_gather x3 -> x0, waiting for transfers between devices: 67.9 us -> none  [grad_rows(): return lax.all_gather(value, 'tensor', axis=0, tiled=True)]
    ppermute x0 -> x9, waiting for transfers between devices: none -> 55.6 us  [the longest x6 55.6 us: change_trails(): lax.ppermute(fresh, chip_axis, [(u, (u + 1) % side_arr) for u in range(si...]
    reduce_scatter x1, waiting for transfers between devices: 66.7 us -> 23.6 us  [shards(): lax.psum_scatter(down_grad, 'dp', scatter_dimension=1, tiled=True)]
    reduce_scatter x1, waiting for transfers between devices: 23.6 us -> 66.7 us  [shards(): lax.psum_scatter(up_grad, 'dp', scatter_dimension=0, tiled=True)]
    squeeze x28, local copies, waits for them, and re-layouts: 8.29 us -> 31.9 us  [attend_all(): lax.map(one_sequence, (split_heads(query, count), split_heads(keys, count...]
    dot_general x16, matrix products: 13.8 us -> 33.4 us  [one_block(): jnp.einsum('qhd,khd->hqk', piece, keys, preferred_element_type=jnp.float32)]
    dot_general x8, matrix products: 12.9 us -> 31.6 us  [one_block(): jnp.einsum('qhd,khd->hqk', grad_piece, values, preferred_element_type=jnp...]
    unnamed x29 -> x26, waiting for transfers between devices: 324 us -> 323 us
  transfers between devices with their start and end apart: 24 -> 30, of which waited for: 20 -> 23; matrix products, arithmetic and copies ran while one was open for 3% -> 3% of each run, Pallas kernels for 0% -> 0%
where the time goes in v1:
time: 1750 us; the launch traced here: 1740 us
  waiting for transfers between devices  936 us (53%)
  blocking collectives  354 us (20%)
  matrix products  203 us (12%)
  local copies, waits for them, and re-layouts  142 us (8%)
  other arithmetic  50.6 us (3%)
  loops' own time  27.5 us (2%)
    unnamed x26, waiting for transfers between devices  323 us
    reduce_scatter x4, waiting for transfers between devices, input_sum(): return lax.psum_scatter(total, 'tensor', scatter_dimension=0, tiled=True)  140 us
    reduce_scatter x3, waiting for transfers between devices, branch_sum(): lax.psum_scatter(jnp.dot(mixed, weight, preferred_element_type=jnp.float3...  133 us
    reduce_scatter x1, waiting for transfers between devices, shards(): lax.psum_scatter(up_grad, 'dp', scatter_dimension=0, tiled=True)  66.7 us
    reduce_scatter x1, waiting for transfers between devices, shards(): lax.psum_scatter(self_output_grad, 'dp', scatter_dimension=1, tiled=True)  65.4 us
    reduce_scatter x1, waiting for transfers between devices, shards(): lax.psum_scatter(cross_output_grad, 'dp', scatter_dimension=1, tiled=True)  64.1 us
    reduce_scatter x1, waiting for transfers between devices, shards(): lax.psum_scatter(cross_query_grad, 'dp', scatter_dimension=0, tiled=True)  64.1 us
    ppermute x6, waiting for transfers between devices, change_trails(): lax.ppermute(fresh, chip_axis, [(u, (u + 1) % side_arr) for u in range(si...  55.6 us
  transfers between devices with their start and end apart: 30, of which 23 were waited for; matrix products, arithmetic and copies ran while one was open for 3% of the time, Pallas kernels for 0%

profile of v1, /device:TPU:0, one launch (start us, length us, event | category | flops | bytes accessed | tf_op | source)
XLA Modules:
  0.0 1736.2 jit_solution(13358180007152276099)
XLA Ops:
  102.1 32.7 %all_gather.46 = bf16[128,512]{0,1:T(8,128)(2,1)} all-gather(bf16[128,64]{0,1:T(8,128)(2,1)} %param.47), channel_id=1, replica_groups=mesh['dp'=8,'tensor'=4] {'dp'}, dimensions={1}, use_global_device_ids=true | all-gather | bytes 147456 | tf_op jit(solution)/shard_map/all_gather | solution.py:275
  152.4 33.2 %while.147 = (s32[]{:T(128)}, bf16[2,1024,2,64]{3,2,1,0:T(2,128)(2,1)S(1)}, f32[2,2,2,512]{3,2,1,0:T(2,128)}, bf16[2,1024,2,64]{1,3,2,0:T(8,128)(2,1)}, bf16[2,1...) while((s32[]{:T(128)}, ...), condition=%wide.region_5.6_spmd, body=%wide.region_0.5_spmd.sunk | while | flops 283720704 | bytes 18707520 | solution.py:196
  189.9 44.5 %reduce-scatter.28.cloned.1.call-done = f32[512,512]{1,0:T(8,128)} async-done(((f32[2048,512]{1,0:T(8,128)}), f32[512,512]{1,0:T(8,128)}) %reduce-scatter.28.cloned.1.call-update) | async-done | bytes 1048592 | tf_op jit(solution)/shard_map/reduce_scatter | solution.py:87
  406.2 44.6 %reduce-scatter.30.cloned.1.call-done = f32[512,512]{1,0:T(8,128)} async-done(((f32[2048,512]{1,0:T(8,128)}), f32[512,512]{1,0:T(8,128)}) %reduce-scatter.30.cloned.1.call-update) | async-done | bytes 1048592 | tf_op jit(solution)/shard_map/reduce_scatter | solution.py:87
  535.4 44.2 %reduce-scatter.32.cloned.1.call-done = f32[512,512]{1,0:T(8,128)} async-done(((f32[2048,512]{1,0:T(8,128)}), f32[512,512]{1,0:T(8,128)}) %reduce-scatter.32.cloned.1.call-update) | async-done | bytes 1048592 | tf_op jit(solution)/shard_map/reduce_scatter | solution.py:87
  621.7 44.4 %reduce-scatter.34.cloned.1.call-done = f32[512,512]{1,0:T(8,128)} async-done(((f32[2048,512]{1,0:T(8,128)}), f32[512,512]{1,0:T(8,128)}) %reduce-scatter.34.cloned.1.call-update) | async-done | bytes 1048592 | tf_op jit(solution)/shard_map/reduce_scatter | solution.py:112
  702.9 87.1 %while.151 = (s32[]{:T(128)}, bf16[2,1024,2,64]{3,2,1,0:T(2,128)(2,1)}, bf16[2,1024,2,64]{1,3,2,0:T(8,128)(2,1)}, bf16[2,1024,2,64]{1,3,2,0:T(8,128)(2,1)}, bf16...) while((s32[]{:T(128)}, ...), condition=%wide.region_30.31_spmd, body=%wide.region_26.30_spmd.sunk | while | flops 684719104 | bytes 73578608 | solution.py:217
  709.7 33.5 %while.156 = (s32[]{:T(128)}, f32[1024,2,64]{0,2,1:T(8,128)S(1)}, f32[1024,2,64]{0,2,1:T(8,128)S(1)}, bf16[2,512,2,64]{1,3,2,0:T(8,128)(2,1)}, s32[2]{0:T(128)S(...) while((s32[]{:T(128)}, f32[1024,2,64]{0,2,1:T(8,128)S(1)}, ...), condition=%wide.region_29.29_spmd.clone, body=%wide.region_27.28_spmd.clone.sunk | while | flops 684456960 | bytes 68580160 | solution.py:180
  753.2 33.5 %while.156 = (s32[]{:T(128)}, f32[1024,2,64]{0,2,1:T(8,128)S(1)}, f32[1024,2,64]{0,2,1:T(8,128)S(1)}, bf16[2,512,2,64]{1,3,2,0:T(8,128)(2,1)}, s32[2]{0:T(128)S(...) while((s32[]{:T(128)}, f32[1024,2,64]{0,2,1:T(8,128)S(1)}, ...), condition=%wide.region_29.29_spmd.clone, body=%wide.region_27.28_spmd.clone.sunk | while | flops 684456960 | bytes 68580160 | solution.py:180
  795.3 44.4 %reduce-scatter.36.cloned.1.call-done = f32[512,512]{1,0:T(8,128)} async-done(((f32[2048,512]{1,0:T(8,128)}), f32[512,512]{1,0:T(8,128)}) %reduce-scatter.36.cloned.1.call-update) | async-done | bytes 1048592 | tf_op jit(solution)/shard_map/reduce_scatter | solution.py:112
  875.5 102.7 %while.153 = (s32[]{:T(128)}, bf16[2,1024,2,64]{3,2,1,0:T(2,128)(2,1)}, bf16[2,1024,2,64]{1,3,2,0:T(8,128)(2,1)}, bf16[2,1024,2,64]{1,3,2,0:T(8,128)(2,1)}, bf16...) while((s32[]{:T(128)}, ...), condition=%wide.region_38.39_spmd, body=%wide.region_34.38_spmd.sunk | while | flops 690502656 | bytes 82012608 | solution.py:217
  882.6 39.8 %while.157 = (s32[]{:T(128)}, f32[1024,2,64]{0,2,1:T(8,128)S(1)}, f32[1024,2,64]{0,2,1:T(8,128)}, bf16[2,512,2,64]{1,3,2,0:T(8,128)(2,1)}, s32[2]{0:T(128)}, /*i...) while((s32[]{:T(128)}, f32[1024,2,64]{0,2,1:T(8,128)S(1)}, ...), condition=%wide.region_37.37_spmd.clone, body=%wide.region_35.36_spmd.clone.sunk | while | flops 690240512 | bytes 77005864 | solution.py:180
  933.8 39.9 %while.157 = (s32[]{:T(128)}, f32[1024,2,64]{0,2,1:T(8,128)S(1)}, f32[1024,2,64]{0,2,1:T(8,128)}, bf16[2,512,2,64]{1,3,2,0:T(8,128)(2,1)}, s32[2]{0:T(128)}, /*i...) while((s32[]{:T(128)}, f32[1024,2,64]{0,2,1:T(8,128)S(1)}, ...), condition=%wide.region_37.37_spmd.clone, body=%wide.region_35.36_spmd.clone.sunk | while | flops 690240512 | bytes 77005864 | solution.py:180
  1036.3 39.9 %all-reduce = (f32[6,512]{1,0:T(8,128)}, f32[2,512]{1,0:T(2,128)S(1)}) all-reduce(f32[6,512]{1,0:T(8,128)S(1)} %stack.36, f32[2,512]{1,0:T(2,128)S(1)} %pad_maximum_fusion), channel_id=1, replica_groups=mesh['dp'=8,'tensor'=4] {'dp','tensor'}, use_global_device_ids=true, to_apply=%region_57.58 | all-reduce | flops 4096 | bytes 32768 | tf_op jit(solution)/shard_map/psum | solution.py:391
  1100.4 66.7 %reduce-scatter.48.cloned.1.call-done = f32[64,512]{1,0:T(8,128)} async-done(((f32[512,512]{1,0:T(8,128)}), f32[64,512]{1,0:T(8,128)}) %reduce-scatter.48.cloned.1.call-update) | async-done | bytes 131088 | tf_op jit(solution)/shard_map/reduce_scatter | solution.py:388
  1167.1 64.1 %reduce-scatter.46.cloned.1.call-done = f32[128,64]{0,1:T(8,128)} async-done(((f32[128,512]{0,1:T(8,128)}), f32[128,64]{0,1:T(8,128)}) %reduce-scatter.46.cloned.1.call-update) | async-done | bytes 32784 | tf_op jit(solution)/shard_map/reduce_scatter | solution.py:387
  1231.3 64.1 %reduce-scatter.44.cloned.1.call-done = f32[64,128]{1,0:T(8,128)} async-done(((f32[512,128]{1,0:T(8,128)}), f32[64,128]{1,0:T(8,128)}) %reduce-scatter.44.cloned.1.call-update) | async-done | bytes 32784 | tf_op jit(solution)/shard_map/reduce_scatter | solution.py:384
  1295.3 64.1 %reduce-scatter.58.cloned.1.call-done = f32[64,128]{1,0:T(8,128)} async-done(((f32[512,128]{1,0:T(8,128)}), f32[64,128]{1,0:T(8,128)}) %reduce-scatter.58.cloned.1.call-update) | async-done | bytes 32784
  1359.4 64.1 %reduce-scatter.60.cloned.1.call-done = f32[64,128]{1,0:T(8,128)} async-done(((f32[512,128]{1,0:T(8,128)}), f32[64,128]{1,0:T(8,128)}) %reduce-scatter.60.cloned.1.call-update) | async-done | bytes 32784
  1423.5 46.5 %reduce-scatter.40.cloned.1.call-done = f32[512,512]{1,0:T(8,128)} async-done(((f32[2048,512]{1,0:T(8,128)}), f32[512,512]{1,0:T(8,128)}) %reduce-scatter.40.cloned.1.call-update) | async-done | bytes 1048592 | tf_op jit(solution)/shard_map/reduce_scatter | solution.py:112
  1469.9 65.4 %reduce-scatter.42.cloned.1.call-done = f32[128,64]{0,1:T(8,128)} async-done(((f32[128,512]{0,1:T(8,128)}), f32[128,64]{0,1:T(8,128)}) %reduce-scatter.42.cloned.1.call-update) | async-done | bytes 32784 | tf_op jit(solution)/shard_map/reduce_scatter | solution.py:383
  1535.3 64.6 %reduce-scatter.54.cloned.1.call-done = f32[64,128]{1,0:T(8,128)} async-done(((f32[512,128]{1,0:T(8,128)}), f32[64,128]{1,0:T(8,128)}) %reduce-scatter.54.cloned.1.call-update) | async-done | bytes 32784
  1599.9 64.4 %reduce-scatter.56.cloned.1.call-done = f32[64,128]{1,0:T(8,128)} async-done(((f32[512,128]{1,0:T(8,128)}), f32[64,128]{1,0:T(8,128)}) %reduce-scatter.56.cloned.1.call-update) | async-done | bytes 32784
  1664.3 64.6 %reduce-scatter.52.cloned.1.call-done = f32[64,128]{1,0:T(8,128)} async-done(((f32[512,128]{1,0:T(8,128)}), f32[64,128]{1,0:T(8,128)}) %reduce-scatter.52.cloned.1.call-update) | async-done | bytes 32784
  (677 shorter events, 833.8 us)
Async XLA Ops:
  7.2 127.6 %all-gather.5.cloned.1.call-start = ((), (), s32[]{:S(2)}) async-start(), calls=%async_computation.17 | async-start | bytes 2621440 | tf_op jit(solution)/shard_map/all_gather | solution.py:79
  7.9 226.5 %reduce-scatter.28.cloned.1.call-start = ((), (), s32[]{:S(2)}) async-start(), calls=%async_computation.18 | async-start | bytes 5242880 | tf_op jit(solution)/shard_map/reduce_scatter | solution.py:87
  188.9 173.7 %all-gather.9.cloned.1.call-start = ((), (), s32[]{:S(2)}) async-start(), calls=%async_computation.20 | async-start | bytes 2621440 | tf_op jit(solution)/shard_map/all_gather | solution.py:79
  189.7 183.6 %all-gather.7.cloned.1.call-start = ((), (), s32[]{:S(2)}) async-start(), calls=%async_computation.19 | async-start | bytes 2621440 | tf_op jit(solution)/shard_map/all_gather | solution.py:79
  238.5 212.4 %reduce-scatter.30.cloned.1.call-start = ((), (), s32[]{:S(2)}) async-start(), calls=%async_computation.21 | async-start | bytes 5242880 | tf_op jit(solution)/shard_map/reduce_scatter | solution.py:87
  406.2 110.8 %all-gather.11.cloned.1.call-start = ((), (), s32[]{:S(2)}) async-start(), calls=%async_computation.22 | async-start | bytes 2621440 | tf_op jit(solution)/shard_map/all_gather | solution.py:79
  453.8 125.8 %reduce-scatter.32.cloned.1.call-start = ((), (), s32[]{:S(2)}) async-start(), calls=%async_computation.23 | async-start | bytes 5242880 | tf_op jit(solution)/shard_map/reduce_scatter | solution.py:87
  534.7 131.3 %reduce-scatter.34.cloned.1.call-start = ((), (), s32[]{:S(2)}) async-start(), calls=%async_computation.24 | async-start | bytes 5242880 | tf_op jit(solution)/shard_map/reduce_scatter | solution.py:112
  585.6 15.9 collective-permute-start.1
  621.7 218.0 %reduce-scatter.36.cloned.1.call-start = ((), (), s32[]{:S(2)}) async-start(), calls=%async_computation.25 | async-start | bytes 5242880 | tf_op jit(solution)/shard_map/reduce_scatter | solution.py:112
  671.7 14.7 collective-permute-start.4
  795.2 237.7 %reduce-scatter.38.cloned.1.call-start = ((), (), s32[]{:S(2)}) async-start(), calls=%async_computation.26 | async-start | bytes 5242880 | tf_op jit(solution)/shard_map/reduce_scatter | solution.py:112
  843.8 14.1 collective-permute-start.7
  988.6 111.9 %reduce-scatter.50.cloned.1.call-start = ((), (), s32[]{:S(2)}) async-start(), calls=%async_computation.32 | async-start | bytes 1179648 | tf_op jit(solution)/shard_map/reduce_scatter | solution.py:389
  994.1 173.0 %reduce-scatter.48.cloned.1.call-start = ((), (), s32[]{:S(2)}) async-start(), calls=%async_computation.31 | async-start | bytes 1179648 | tf_op jit(solution)/shard_map/reduce_scatter | solution.py:388
  999.0 232.3 %reduce-scatter.46.cloned.1.call-start = ((), (), s32[]{:S(2)}) async-start(), calls=%async_computation.30 | async-start | bytes 294912 | tf_op jit(solution)/shard_map/reduce_scatter | solution.py:387
  1002.5 292.8 %reduce-scatter.44.cloned.1.call-start = ((), (), s32[]{:S(2)}) async-start(), calls=%async_computation.29 | async-start | bytes 294912 | tf_op jit(solution)/shard_map/reduce_scatter | solution.py:384
  1005.6 353.8 %reduce-scatter.58.cloned.1.call-start = ((), (), s32[]{:S(2)}) async-start(), calls=%async_computation.36 | async-start | bytes 294912
  1008.7 414.7 %reduce-scatter.60.cloned.1.call-start = ((), (), s32[]{:S(2)}) async-start(), calls=%async_computation.37 | async-start | bytes 294912
  1013.5 456.5 %reduce-scatter.40.cloned.1.call-start = ((), (), s32[]{:S(2)}) async-start(), calls=%async_computation.27 | async-start | bytes 5242880 | tf_op jit(solution)/shard_map/reduce_scatter | solution.py:112
  1017.0 518.3 %reduce-scatter.42.cloned.1.call-start = ((), (), s32[]{:S(2)}) async-start(), calls=%async_computation.28 | async-start | bytes 294912 | tf_op jit(solution)/shard_map/reduce_scatter | solution.py:383
  1021.3 578.5 %reduce-scatter.54.cloned.1.call-start = ((), (), s32[]{:S(2)}) async-start(), calls=%async_computation.34 | async-start | bytes 294912
  1023.1 641.2 %reduce-scatter.56.cloned.1.call-start = ((), (), s32[]{:S(2)}) async-start(), calls=%async_computation.35 | async-start | bytes 294912
  1025.5 703.3 %reduce-scatter.52.cloned.1.call-start = ((), (), s32[]{:S(2)}) async-start(), calls=%async_computation.33 | async-start | bytes 294912
  (127 other events, 2914.9 us)
Sparse Core Ops, SparseCore 0:
  9.6 25.2 all-gather.4
  189.0 45.3 reduce-scatter.27
  236.1 22.5 all-gather.8
  260.8 22.5 all-gather.6
  406.3 44.5 reduce-scatter.29
  453.9 22.5 all-gather.10
  534.8 44.6 reduce-scatter.31
  621.8 44.2 reduce-scatter.33
  795.3 44.2 reduce-scatter.35
  988.7 44.1 reduce-scatter.37
  1036.9 63.4 reduce-scatter.49
  1104.7 62.4 reduce-scatter.47
  1171.0 60.2 reduce-scatter.45
  1235.0 60.2 reduce-scatter.43
  1299.1 60.2 reduce-scatter.57
  1363.2 60.2 reduce-scatter.59
  1426.4 43.4 reduce-scatter.39
  1474.1 61.2 reduce-scatter.41
  1539.6 60.2 reduce-scatter.53
  1604.0 60.2 reduce-scatter.55
  1668.5 60.2 reduce-scatter.51
